TPU v7x, 32 devices: a whole 2x2x4 slice. The times are simulated.
32 devices in a mesh: obs: 16 (over z, x, core), sp: 2 (over y).
Axes of the slice: x: 2, y: 2, z: 4, core: 2. Of those that a mesh axis runs over, the one named last changes fastest.
Arguments:
- descriptors: bfloat16 [16384, 512], P('obs'), may hold values from -10 to 10
- candidates: bfloat16 [8192, 512], P('obs'), may hold values from -10 to 10
- sparse_index: int32 [4096], replicated, may hold values from 0 to 8191, as said below
- targets: bfloat16 [16384], P('obs'), may hold values from -12 to 12
- regularizer: float32 [4096], replicated, may hold values from 0.25 to 1
Outputs:
- inverse: float32 [4096, 4096], P('sp', 'obs')
- weights: float32 [4096], P('sp')
Inputs may be any that keep to these rules, and one draw needn't show every extreme that they name: `sparse_index`: the 4096 indices are distinct.
All inputs are finite; a program needn't handle non-finite values.
Results may differ from a plain program's by a relative error of at most 0.012.
Values may be sent and summed in bfloat16 or wider, within the bound.
A program may use at most 128 MiB of HBM per device.

v0:
```python
import math
import jax
import jax.numpy as jnp
from jax import lax
from jax.sharding import PartitionSpec as P

epsilon = 1e-06


def unit_rows(row_block):
    values = row_block.astype(jnp.float32)
    return (values * lax.rsqrt(jnp.sum(values * values, axis=1, keepdims=True) + epsilon)).astype(
        jnp.bfloat16
    )


def kernel_block(normed, sparse):
    inner = lax.dot_general(
        normed, sparse, (((1,), (1,)), ((), ())), preferred_element_type=jnp.float32
    )
    scaled = inner * math.sqrt(normed.shape[1])
    squared = scaled * scaled
    return (squared * squared - 6.0 * squared + 3.0).astype(jnp.bfloat16)


def select_rows(candidate_units, wanted, cand_start):
    shifted = wanted - cand_start
    inside = (shifted >= 0) & (shifted < candidate_units.shape[0])
    picked = candidate_units[jnp.clip(shifted, 0, candidate_units.shape[0] - 1)].astype(jnp.float32)
    return picked * inside[:, None].astype(jnp.float32)


def first_iterate(system_part, row_scale, col_scale, on_diag):
    return (
        jnp.where(on_diag, 2.0 * row_scale[:, None], 0.0)
        - system_part * row_scale[:, None] * col_scale[None, :]
    )


def on_device(descriptors, candidates, sparse_index, targets, regularizer):
    obs_count = lax.axis_size("obs")
    sp_count = lax.axis_size("sp")
    obs_pos = lax.axis_index("obs")
    sp_pos = lax.axis_index("sp")
    sparse_count = sparse_index.shape[0]
    block_rows = sparse_count // sp_count
    tile_cols = sparse_count // obs_count
    rows_all = descriptors.shape[0] * obs_count
    normed = unit_rows(descriptors)
    candidate_units = unit_rows(candidates)
    cand_start = obs_pos * candidates.shape[0]
    all_sparse = lax.psum(
        select_rows(candidate_units, sparse_index, cand_start).astype(jnp.bfloat16), "obs"
    )
    full_kernel = kernel_block(normed, all_sparse)
    own_kernel = lax.dynamic_slice_in_dim(full_kernel, sp_pos * block_rows, block_rows, 1)
    gram_part = lax.psum_scatter(
        lax.dot_general(
            full_kernel, own_kernel, (((0,), (0,)), ((), ())), preferred_element_type=jnp.float32
        ),
        "obs",
        scatter_dimension=0,
        tiled=True,
    )
    weighted = jnp.dot(targets, own_kernel, preferred_element_type=jnp.float32)
    squares = jnp.sum(jnp.square(own_kernel.astype(jnp.float32)), axis=0)
    weighted, squares = lax.psum((weighted, squares), "obs")
    weighted, squares = (
        lax.all_gather(weighted, "sp", axis=0, tiled=True),
        lax.all_gather(squares, "sp", axis=0, tiled=True),
    )
    normalizer = 24.0 * rows_all
    projected = weighted / math.sqrt(normalizer)
    recip = 1.0 / (squares / normalizer + regularizer)
    row_ids = sp_pos * block_rows + lax.iota(jnp.int32, block_rows)
    col_ids = obs_pos * tile_cols + lax.iota(jnp.int32, tile_cols)
    all_ids = lax.iota(jnp.int32, sparse_count)
    on_diag = row_ids[:, None] == col_ids[None, :]
    reg_rows = lax.dynamic_slice_in_dim(regularizer, sp_pos * block_rows, block_rows)
    recip_rows = lax.dynamic_slice_in_dim(recip, sp_pos * block_rows, block_rows)
    recip_cols = lax.dynamic_slice_in_dim(recip, obs_pos * tile_cols, tile_cols)
    system_tile = gram_part.T / normalizer + jnp.where(on_diag, reg_rows[:, None], 0.0)
    highest = lax.Precision.HIGHEST
    system_full_rows = lax.all_gather(system_tile, "obs", axis=1, tiled=True)
    system_full_cols = lax.all_gather(system_tile, "sp", axis=0, tiled=True)
    first_rows = first_iterate(
        system_full_rows, recip_rows, recip, row_ids[:, None] == all_ids[None, :]
    )
    first_cols = first_iterate(
        system_full_cols, recip, recip_cols, all_ids[:, None] == col_ids[None, :]
    )
    product_tile = jnp.dot(system_full_rows, first_cols, precision=highest)
    product_full_cols = lax.all_gather(product_tile, "sp", axis=0, tiled=True)
    first_tile = first_iterate(system_tile, recip_rows, recip_cols, on_diag)
    inverse_tile = 2.0 * first_tile - jnp.dot(first_rows, product_full_cols, precision=highest)
    projected_cols = lax.dynamic_slice_in_dim(projected, obs_pos * tile_cols, tile_cols)
    weight_part = jnp.dot(inverse_tile, projected_cols, precision=highest)
    weights = lax.psum(weight_part, "obs")
    return (inverse_tile, weights)


def solution(mesh):
    in_specs = (P("obs", None), P("obs", None), P(), P("obs"), P())
    out_specs = (P("sp", "obs"), P("sp"))
    return jax.shard_map(
        on_device, mesh=mesh, in_specs=in_specs, out_specs=out_specs, check_vma=False
    )
```

profile of v0, /device:TPU:0, one launch (start us, length us, event | category | flops | bytes accessed | tf_op | source)
XLA Modules:
  0.0 955.4 jit_solution(15224427852561429307)
XLA Ops:
  7.2 0.0 all-reduce.3.cloned.1.call-start
  7.2 0.7 fusion.36
  7.9 0.7 and_convert_fusion
  8.7 1.2 fusion.32
  9.9 1.2 fusion.33
  11.1 17.3 %gather_fusion = bf16[4096,512]{1,0:T(8,128)(2,1)} fusion(bf16[512,512]{1,0:T(8,128)(2,1)S(1)} %fusion.33, s32[4096]{0:T(1024)S(1)} %fusion.36), kind=kCustom, calls=%fused_computation | custom fusion | bytes 8404992 | tf_op jit(solution)/shard_map/gather | solution.py:29
  28.4 4.0 multiply_convert_fusion
  32.5 0.0 copy-start.3
  32.5 0.0 all-reduce.3.cloned.1.call-update
  32.5 0.0 reduce-scatter.2.cloned.1.call-start
  32.6 1.1 copy-done.3
  33.7 0.3 fusion.22
  34.0 112.7 %all-reduce.3.cloned.1.call-done = bf16[4096,512]{1,0:T(8,128)(2,1)} async-done(((bf16[4096,512]{1,0:T(8,128)(2,1)}), bf16[4096,512]{1,0:T(8,128)(2,1)}) %all-reduce.3.cloned.1.call-update) | async-done | bytes 4194320 | tf_op jit(solution)/shard_map/psum | solution.py:52
  146.7 7.7 add_convert_fusion
  154.4 0.0 copy-start.2
  154.4 3.2 copy-done.2
  157.6 22.4 %fusion.17 = f32[4096,2048]{1,0:T(8,128)} fusion(bf16[1024,4096]{1,0:T(8,128)(2,1)S(1)} %add_convert_fusion, s32[]{:T(128)} %select_n.28), kind=kOutput, calls=%fused_computation.23 | convolution fusion | flops 17179869184 | bytes 46137348 | tf_op jit(solution)/shard_map/dot_general | solution.py:58
  180.0 0.0 dynamic-slice-start
  180.0 0.0 reduce-scatter.2.cloned.1.call-update
  180.1 0.0 all-gather.6.cloned.1.call-start
  180.1 0.0 copy-start.5
  180.2 331.8 %reduce-scatter.2.cloned.1.call-done = f32[256,2048]{1,0:T(8,128)} async-done(((f32[4096,2048]{1,0:T(8,128)}), f32[256,2048]{1,0:T(8,128)}) %reduce-scatter.2.cloned.1.call-update) | async-done | bytes 2097168 | tf_op jit(solution)/shard_map/reduce_scatter | solution.py:57
  512.0 0.0 dynamic-slice-done
  512.0 3.3 fusion.26
  515.2 0.0 all-gather.6.cloned.1.call-update
  515.3 0.0 all-gather.4.cloned.1.call-start
  515.3 0.5 all-gather.4.cloned.1.call-update
  515.9 0.0 all-gather.8.cloned.1.call-start
  515.9 0.0 copy-done.5
  515.9 0.0 copy-start.4
  515.9 3.1 multiply_reduce_fusion
  519.0 3.3 fusion.15
  522.3 59.1 %all-reduce = (f32[2048]{0:T(1024)S(1)}, f32[2048]{0:T(1024)S(1)}) all-reduce(f32[2048]{0:T(1024)S(1)} %multiply_reduce_fusion, f32[2048]{0:T(1024)S(1)} %bitcast.13), channel_id=1, replica_groups=mesh['obs'=16,'sp'=2] {'obs'}, use_global_device_ids=true, to_apply=%region_4.5 | all-reduce | flops 4096 | bytes 32768 | tf_op jit(solution)/shard_map/psum | solution.py:67
  581.4 4.4 all_gather.15
  585.7 0.0 copy-done.4
  585.7 0.1 dynamic_slice.18
  585.8 0.0 all-gather.6.cloned.1.call-done
  585.8 155.6 %all-gather.4.cloned.1.call-done = f32[2048,4096]{0,1:T(8,128)} async-done(((f32[2048,256]{0,1:T(8,128)}), f32[2048,4096]{0,1:T(8,128)}) %all-gather.4.cloned.1.call-update) | async-done | bytes 33554448 | tf_op jit(solution)/shard_map/all_gather | solution.py:84
  741.4 0.0 copy-start
  741.4 67.7 %fusion.10 = f32[2048,256]{1,0:T(8,128)} fusion(f32[2048,4096]{0,1:T(8,128)} %all-gather.4.cloned.1.call-done, f32[4096,256]{0,1:T(8,128)} %all-gather.6.cloned.1.call-done, f32[256]{0:T(256)S(1)} %dynamic_slice.18, f32[4096]{0:T(1024)S(1)} %get-tuple-element.11, f32[4096]{0:T(1024)S(1)} %get-tuple-element.10, s32[256]{0:T(256)S(1)} %iota_add_fusion.1), kind=kOutput, calls=%fused_computation.15 | convolution fusion | flops 25775046656 | bytes 39880704 | tf_op jit(solution)/shard_map/dot_general | solution.py:92
  809.1 0.0 all-gather.8.cloned.1.call-update
  809.1 4.4 all_gather.19
  813.4 0.1 dynamic-slice_multiply_fusion
  813.5 52.5 %all-gather.8.cloned.1.call-done = f32[4096,256]{1,0:T(8,128)} async-done(((f32[2048,256]{1,0:T(8,128)}), f32[4096,256]{1,0:T(8,128)}) %all-gather.8.cloned.1.call-update) | async-done | bytes 4194320 | tf_op jit(solution)/shard_map/all_gather | solution.py:93
  866.0 0.0 copy-done
  866.0 44.1 %fusion.19 = f32[2048,256]{0,1:T(8,128)} fusion(f32[4096,256]{1,0:T(8,128)} %all-gather.8.cloned.1.call-done, f32[2048,4096]{0,1:T(8,128)} %all-gather.4.cloned.1.call-done, f32[4096]{0:T(1024)S(1)} %get-tuple-element.11, f32[2048]{0:T(1024)S(1)} %get-tuple-element.9, f32[2048]{0:T(1024)S(1)} %get-tuple-element.8, s32[2048]{0:T(1024)S(1)} %iota_add_fusion, ...), kind=kOutput, calls=%fused_computation.25 | convolution fusion | flops 25815416832 | bytes 41986048 | tf_op jit(solution)/shard_map/dot_general | solution.py:95
  910.1 0.0 copy-start.1
  910.1 3.0 copy.10
  913.1 0.0 copy-done.1
  913.1 1.2 fusion.41
  914.3 34.2 %psum.31 = f32[2048]{0:T(1024)} all-reduce(f32[2048]{0:T(1024)S(1)} %bitcast.12), channel_id=1, replica_groups=mesh['obs'=16,'sp'=2] {'obs'}, use_global_device_ids=true, to_apply=%region_7.8 | all-reduce | flops 2048 | bytes 16384 | tf_op jit(solution)/shard_map/psum | solution.py:98
  (7 shorter events, 0.0 us)
Async XLA Ops:
  7.2 139.6 %all-reduce.3.cloned.1.call-start = ((), (), s32[]{:S(2)}) async-start(), calls=%async_computation.1 | async-start | bytes 8388608 | tf_op jit(solution)/shard_map/psum | solution.py:52
  32.5 1.2 copy-start.3
  32.5 479.5 %reduce-scatter.2.cloned.1.call-start = ((), (), s32[]{:S(2)}) async-start(), calls=%async_computation.2 | async-start | bytes 35651584 | tf_op jit(solution)/shard_map/reduce_scatter | solution.py:57
  154.4 3.2 copy-start.2
  180.0 331.9 %dynamic-slice-start = ((f32[4096]{0:T(1024)}, s32[]{:T(128)}), f32[2048]{0:T(1024)S(1)}, s32[]{:S(2)}) async-start(f32[4096]{0:T(1024)} %param.9, s32[]{:T(128)} %select_n.28), calls=%async_computation.6 | async-start | bytes 16896 | tf_op jit(solution)/shard_map/dynamic_slice | solution.py:79
  180.1 405.7 %all-gather.6.cloned.1.call-start = ((), (), s32[]{:S(2)}) async-start(), calls=%async_computation.4 | async-start | bytes 6291456 | tf_op jit(solution)/shard_map/all_gather | solution.py:85
  180.1 335.8 %copy-start.5 = (bf16[1024]{0:T(1024)(128)(2,1)S(1)}, bf16[1024]{0:T(1024)(128)(2,1)}, u32[]{:S(2)}) copy-start(bf16[1024]{0:T(1024)(128)(2,1)} %param.8) | copy-start | bytes 6148
  515.3 226.1 %all-gather.4.cloned.1.call-start = ((), (), s32[]{:S(2)}) async-start(), calls=%async_computation.3 | async-start | bytes 35651584 | tf_op jit(solution)/shard_map/all_gather | solution.py:84
  515.9 350.1 %all-gather.8.cloned.1.call-start = ((), (), s32[]{:S(2)}) async-start(), calls=%async_computation.5 | async-start | bytes 6291456 | tf_op jit(solution)/shard_map/all_gather | solution.py:93
  515.9 69.8 %copy-start.4 = (f32[4096]{0:T(1024)S(1)}, f32[4096]{0:T(1024)}, u32[]{:S(2)}) copy-start(f32[4096]{0:T(1024)} %param.9) | copy-start | bytes 49156
  741.4 124.6 %copy-start = (f32[2048,256]{0,1:T(8,128)S(1)}, f32[2048,256]{0,1:T(8,128)}, u32[]{:S(2)}) copy-start(f32[2048,256]{0,1:T(8,128)} %fusion.26) | copy-start | bytes 6291460
  910.1 3.0 copy-start.1
Sparse Core Ops, SparseCore 0:
  32.6 114.0 all-reduce.2
  180.2 331.7 reduce-scatter.1
  515.4 55.7 all-gather.5
  573.3 168.0 all-gather.3
  809.2 56.7 all-gather.7
where the time goes:
time: 964 us; the launch traced here: 955 us
  waiting for transfers between devices  653 us (68%)
  matrix products  146 us (15%)
  blocking collectives  102 us (11%)
  local copies, waits for them, and re-layouts  24.8 us (3%)
  other arithmetic  14.6 us (2%)
  between operations  14.3 us (1%)
    reduce_scatter x1, waiting for transfers between devices, on_device(): lax.psum_scatter(lax.dot_general(full_kernel, own_kernel, (((0,), (0,)),...  332 us
    all_gather x1, waiting for transfers between devices, on_device(): system_full_rows = lax.all_gather(system_tile, 'obs', axis=1, tiled=True)  156 us
    psum x1, waiting for transfers between devices, on_device(): lax.psum(select_rows(candidate_units, sparse_index, cand_start).astype(jn...  113 us
    dot_general x1, matrix products, on_device(): product_tile = jnp.dot(system_full_rows, first_cols, precision=highest)  67.7 us
    psum x1, blocking collectives, on_device(): weighted, squares = lax.psum((weighted, squares), 'obs')  59.1 us
    all_gather x1, waiting for transfers between devices, on_device(): product_full_cols = lax.all_gather(product_tile, 'sp', axis=0, tiled=True)  52.5 us
    dot_general x1, matrix products, on_device(): jnp.dot(first_rows, product_full_cols, precision=highest)  44.1 us
    psum x1, blocking collectives, on_device(): weights = lax.psum(weight_part, 'obs')  34.2 us
  transfers between devices with their start and end apart: 5, of which 4 were waited for; matrix products, arithmetic and copies ran while one was open for 1% of the time, Pallas kernels for 0%

commit v1 on v0

--- a/solution.py
+++ b/solution.py
@@ -5,6 +5,12 @@
 from jax.sharding import PartitionSpec as P
 
 epsilon = 1e-06
+
+
+def summed_here(block, mesh_axis):
+    blocks = lax.all_gather(block, mesh_axis, axis=0, tiled=False)
+    total = blocks.sum(axis=0)
+    return total
 
 
 def unit_rows(row_block):
@@ -49,7 +55,7 @@
     normed = unit_rows(descriptors)
     candidate_units = unit_rows(candidates)
     cand_start = obs_pos * candidates.shape[0]
-    all_sparse = lax.psum(
+    all_sparse = summed_here(
         select_rows(candidate_units, sparse_index, cand_start).astype(jnp.bfloat16), "obs"
     )
     full_kernel = kernel_block(normed, all_sparse)

time: 964 us -> 1200 us (1.24)
  waiting for transfers between devices: 653 us -> 869 us
  other arithmetic: 14.6 us -> 38.3 us
    all_gather x0 -> x1, waiting for transfers between devices: none -> 327 us  [summed_here(): blocks = lax.all_gather(block, mesh_axis, axis=0, tiled=False)]
    psum x1 -> x0, waiting for transfers between devices: 113 us -> none  [on_device(): lax.psum(select_rows(candidate_units, sparse_index, cand_start).astype(jn...]
    reduce_sum x0 -> x1, other arithmetic: none -> 23.7 us  [summed_here(): total = blocks.sum(axis=0)]
where the time goes in v1:
time: 1200 us; the launch traced here: 1190 us
  waiting for transfers between devices  869 us (72%)
  matrix products  146 us (12%)
  blocking collectives  102 us (8%)
  other arithmetic  38.3 us (3%)
  local copies, waits for them, and re-layouts  24.8 us (2%)
  between operations  14.3 us (1%)
    reduce_scatter x1, waiting for transfers between devices, on_device(): lax.psum_scatter(lax.dot_general(full_kernel, own_kernel, (((0,), (0,)),...  333 us
    all_gather x1, waiting for transfers between devices, summed_here(): blocks = lax.all_gather(block, mesh_axis, axis=0, tiled=False)  327 us
    all_gather x1, waiting for transfers between devices, on_device(): system_full_rows = lax.all_gather(system_tile, 'obs', axis=1, tiled=True)  155 us
    dot_general x1, matrix products, on_device(): product_tile = jnp.dot(system_full_rows, first_cols, precision=highest)  67.7 us
    psum x1, blocking collectives, on_device(): weighted, squares = lax.psum((weighted, squares), 'obs')  59.2 us
    all_gather x1, waiting for transfers between devices, on_device(): product_full_cols = lax.all_gather(product_tile, 'sp', axis=0, tiled=True)  52.5 us
    dot_general x1, matrix products, on_device(): jnp.dot(first_rows, product_full_cols, precision=highest)  44.1 us
    psum x1, blocking collectives, on_device(): weights = lax.psum(weight_part, 'obs')  34.2 us
  transfers between devices with their start and end apart: 5, of which 4 were waited for; matrix products, arithmetic and copies ran while one was open for 1% of the time, Pallas kernels for 0%

profile of v1, /device:TPU:0, one launch (start us, length us, event | category | flops | bytes accessed | tf_op | source)
XLA Modules:
  0.0 1194.6 jit_solution(12440192629246548952)
XLA Ops:
  7.2 0.0 all-gather.5.cloned.1.call-start
  7.2 0.7 fusion.37
  7.9 0.7 and_convert_fusion
  8.7 1.2 fusion.33
  9.9 1.2 fusion.34
  11.1 17.3 %gather_fusion = bf16[4096,512]{1,0:T(8,128)(2,1)} fusion(bf16[512,512]{1,0:T(8,128)(2,1)S(1)} %fusion.34, s32[4096]{0:T(1024)S(1)} %fusion.37), kind=kCustom, calls=%fused_computation | custom fusion | bytes 8404992 | tf_op jit(solution)/shard_map/gather | solution.py:35
  28.4 4.0 fusion.10
  32.4 0.0 copy-start.3
  32.4 0.0 all-gather.5.cloned.1.call-update
  32.5 0.0 reduce-scatter.2.cloned.1.call-start
  32.5 1.1 copy-done.3
  33.7 0.3 fusion.23
  33.9 327.5 %all-gather.5.cloned.1.call-done = bf16[16,4096,512]{2,1,0:T(8,128)(2,1)} async-done(((bf16[1,4096,512]{2,1,0:T(8,128)(2,1)}), bf16[16,4096,512]{2,1,0:T(8,128)(2,1)}) %all-gather.5.cloned.1.call-update) | async-done | bytes 67108880 | tf_op jit(solution)/shard_map/all_gather | solution.py:11
  361.4 23.7 %reduce_sum.41 = bf16[4096,512]{1,0:T(8,128)(2,1)} reduce(bf16[16,4096,512]{2,1,0:T(8,128)(2,1)} %all-gather.5.cloned.1.call-done, bf16[]{:T(256)} %constant.11.clone.1), dimensions={0}, to_apply=%region_2.3 | reduce | flops 31457280 | bytes 71303168 | tf_op jit(solution)/shard_map/reduce_sum | solution.py:12
  385.1 7.7 add_convert_fusion
  392.8 0.0 copy-start.2
  392.8 3.2 copy-done.2
  396.0 22.4 %fusion.18 = f32[4096,2048]{1,0:T(8,128)} fusion(bf16[1024,4096]{1,0:T(8,128)(2,1)S(1)} %add_convert_fusion, s32[]{:T(128)} %select_n.28), kind=kOutput, calls=%fused_computation.24 | convolution fusion | flops 17179869184 | bytes 46137348 | tf_op jit(solution)/shard_map/dot_general | solution.py:64
  418.4 0.0 dynamic-slice-start
  418.4 0.0 reduce-scatter.2.cloned.1.call-update
  418.4 0.0 all-gather.9.cloned.1.call-start
  418.5 0.0 copy-start.5
  418.5 332.7 %reduce-scatter.2.cloned.1.call-done = f32[256,2048]{1,0:T(8,128)} async-done(((f32[4096,2048]{1,0:T(8,128)}), f32[256,2048]{1,0:T(8,128)}) %reduce-scatter.2.cloned.1.call-update) | async-done | bytes 2097168 | tf_op jit(solution)/shard_map/reduce_scatter | solution.py:63
  751.2 0.0 dynamic-slice-done
  751.2 3.3 fusion.27
  754.4 0.0 all-gather.9.cloned.1.call-update
  754.4 0.0 all-gather.7.cloned.1.call-start
  754.5 0.5 all-gather.7.cloned.1.call-update
  755.0 0.0 all-gather.11.cloned.1.call-start
  755.1 0.0 copy-done.5
  755.1 0.0 copy-start.4
  755.1 3.1 multiply_reduce_fusion
  758.2 3.3 fusion.16
  761.4 59.2 %all-reduce = (f32[2048]{0:T(1024)S(1)}, f32[2048]{0:T(1024)S(1)}) all-reduce(f32[2048]{0:T(1024)S(1)} %multiply_reduce_fusion, f32[2048]{0:T(1024)S(1)} %bitcast.16), channel_id=1, replica_groups=mesh['obs'=16,'sp'=2] {'obs'}, use_global_device_ids=true, to_apply=%region_4.5 | all-reduce | flops 4096 | bytes 32768 | tf_op jit(solution)/shard_map/psum | solution.py:73
  820.6 4.4 all_gather.20
  825.0 0.0 copy-done.4
  825.0 0.1 dynamic_slice.18
  825.1 0.0 all-gather.9.cloned.1.call-done
  825.1 155.5 %all-gather.7.cloned.1.call-done = f32[2048,4096]{0,1:T(8,128)} async-done(((f32[2048,256]{0,1:T(8,128)}), f32[2048,4096]{0,1:T(8,128)}) %all-gather.7.cloned.1.call-update) | async-done | bytes 33554448 | tf_op jit(solution)/shard_map/all_gather | solution.py:90
  980.5 0.0 copy-start
  980.5 67.7 %fusion.11 = f32[2048,256]{1,0:T(8,128)} fusion(f32[2048,4096]{0,1:T(8,128)} %all-gather.7.cloned.1.call-done, f32[4096,256]{0,1:T(8,128)} %all-gather.9.cloned.1.call-done, f32[256]{0:T(256)S(1)} %dynamic_slice.18, f32[4096]{0:T(1024)S(1)} %get-tuple-element.11, f32[4096]{0:T(1024)S(1)} %get-tuple-element.10, s32[256]{0:T(256)S(1)} %iota_add_fusion.1), kind=kOutput, calls=%fused_computation.16 | convolution fusion | flops 25775046656 | bytes 39880704 | tf_op jit(solution)/shard_map/dot_general | solution.py:98
  1048.2 0.0 all-gather.11.cloned.1.call-update
  1048.2 4.4 all_gather.24
  1052.6 0.1 dynamic-slice_multiply_fusion
  1052.7 52.5 %all-gather.11.cloned.1.call-done = f32[4096,256]{1,0:T(8,128)} async-done(((f32[2048,256]{1,0:T(8,128)}), f32[4096,256]{1,0:T(8,128)}) %all-gather.11.cloned.1.call-update) | async-done | bytes 4194320 | tf_op jit(solution)/shard_map/all_gather | solution.py:99
  1105.1 0.0 copy-done
  1105.1 44.1 %fusion.20 = f32[2048,256]{0,1:T(8,128)} fusion(f32[4096,256]{1,0:T(8,128)} %all-gather.11.cloned.1.call-done, f32[2048,4096]{0,1:T(8,128)} %all-gather.7.cloned.1.call-done, f32[4096]{0:T(1024)S(1)} %get-tuple-element.11, f32[2048]{0:T(1024)S(1)} %get-tuple-element.9, f32[2048]{0:T(1024)S(1)} %get-tuple-element.8, s32[2048]{0:T(1024)S(1)} %iota_add_fusion, ...), kind=kOutput, calls=%fused_computation.26 | convolution fusion | flops 25815416832 | bytes 41986048 | tf_op jit(solution)/shard_map/dot_general | solution.py:101
  1149.2 0.0 copy-start.1
  1149.2 3.0 copy.10
  1152.2 0.0 copy-done.1
  1152.2 1.2 fusion.42
  1153.4 34.2 %psum.23 = f32[2048]{0:T(1024)} all-reduce(f32[2048]{0:T(1024)S(1)} %bitcast.15), channel_id=1, replica_groups=mesh['obs'=16,'sp'=2] {'obs'}, use_global_device_ids=true, to_apply=%region_7.8 | all-reduce | flops 2048 | bytes 16384 | tf_op jit(solution)/shard_map/psum | solution.py:104
  (7 shorter events, 0.0 us)
Async XLA Ops:
  7.2 354.2 %all-gather.5.cloned.1.call-start = ((), (), s32[]{:S(2)}) async-start(), calls=%async_computation.1 | async-start | bytes 71303168 | tf_op jit(solution)/shard_map/all_gather | solution.py:11
  32.4 1.2 copy-start.3
  32.5 718.7 %reduce-scatter.2.cloned.1.call-start = ((), (), s32[]{:S(2)}) async-start(), calls=%async_computation.2 | async-start | bytes 35651584 | tf_op jit(solution)/shard_map/reduce_scatter | solution.py:63
  392.8 3.2 copy-start.2
  418.4 332.8 %dynamic-slice-start = ((f32[4096]{0:T(1024)}, s32[]{:T(128)}), f32[2048]{0:T(1024)S(1)}, s32[]{:S(2)}) async-start(f32[4096]{0:T(1024)} %param.9, s32[]{:T(128)} %select_n.28), calls=%async_computation.6 | async-start | bytes 16896 | tf_op jit(solution)/shard_map/dynamic_slice | solution.py:85
  418.4 406.6 %all-gather.9.cloned.1.call-start = ((), (), s32[]{:S(2)}) async-start(), calls=%async_computation.4 | async-start | bytes 6291456 | tf_op jit(solution)/shard_map/all_gather | solution.py:91
  418.5 336.6 %copy-start.5 = (bf16[1024]{0:T(1024)(128)(2,1)S(1)}, bf16[1024]{0:T(1024)(128)(2,1)}, u32[]{:S(2)}) copy-start(bf16[1024]{0:T(1024)(128)(2,1)} %param.8) | copy-start | bytes 6148
  754.4 226.1 %all-gather.7.cloned.1.call-start = ((), (), s32[]{:S(2)}) async-start(), calls=%async_computation.3 | async-start | bytes 35651584 | tf_op jit(solution)/shard_map/all_gather | solution.py:90
  755.0 350.1 %all-gather.11.cloned.1.call-start = ((), (), s32[]{:S(2)}) async-start(), calls=%async_computation.5 | async-start | bytes 6291456 | tf_op jit(solution)/shard_map/all_gather | solution.py:99
  755.1 69.9 %copy-start.4 = (f32[4096]{0:T(1024)S(1)}, f32[4096]{0:T(1024)}, u32[]{:S(2)}) copy-start(f32[4096]{0:T(1024)} %param.9) | copy-start | bytes 49156
  980.5 124.6 %copy-start = (f32[2048,256]{0,1:T(8,128)S(1)}, f32[2048,256]{0,1:T(8,128)}, u32[]{:S(2)}) copy-start(f32[2048,256]{0,1:T(8,128)} %fusion.27) | copy-start | bytes 6291460
  1149.2 3.0 copy-start.1
Sparse Core Ops, SparseCore 0:
  32.6 328.7 all-gather.4
  418.5 332.5 reduce-scatter.1
  754.6 55.8 all-gather.8
  812.4 168.0 all-gather.6
  1048.4 56.7 all-gather.10
